TPU v7x, 32 devices: a whole 2x2x4 slice. The times are simulated.
32 devices in a mesh: dp: 8 (over y, x, core), tensor: 4 (over z).
Axes of the slice: x: 2, y: 2, z: 4, core: 2. Of those that a mesh axis runs over, the one named last changes fastest.
Arguments:
- inputs: bfloat16 [16, 1024, 1024], P('dp', 'tensor'), may hold values from -6 to 6
- cotangent: bfloat16 [16, 1024, 1024], P('dp', 'tensor'), may hold values from -6 to 6
- lengths: int32 [16], P('dp'), may hold values from 1 to 1024, as said below
- block_ids: int32 [16, 1024], P('dp'), may hold values from 0 to 7, never falling along the last dimension, each value on 1 to 256 neighbouring positions
- ln1_gain: float32 [1024], replicated, may hold values from 0.5 to 1.5
- ln1_bias: float32 [1024], replicated, may hold values from -1 to 1
- ln2_gain: float32 [1024], replicated, may hold values from 0.5 to 1.5
- ln2_bias: float32 [1024], replicated, may hold values from -1 to 1
- w_qkv: bfloat16 [1024, 3072], P('dp', 'tensor'), may hold values from -0.1875 to 0.1875
- b_qkv: float32 [3072], P('tensor'), may hold values from -1 to 1
- w_out: bfloat16 [1024, 1024], P('dp', 'tensor'), may hold values from -1 to 1
- b_out: float32 [1024], replicated, may hold values from -1 to 1
- w_up: bfloat16 [1024, 4096], P('dp', 'tensor'), may hold values from -0.1875 to 0.1875
- b_up: float32 [4096], P('tensor'), may hold values from -1 to 1
- w_down: bfloat16 [1024, 4096], P('dp', 'tensor'), may hold values from -0.09375 to 0.09375
- b_down: float32 [1024], replicated, may hold values from -1 to 1
Outputs:
- layer_out: bfloat16 [16, 1024, 1024], P('dp', 'tensor')
- grad_inputs: float32 [16, 1024, 1024], P('dp', 'tensor')
- grad_w_qkv: float32 [1024, 3072], P('dp', 'tensor')
- grad_w_out: float32 [1024, 1024], P('dp', 'tensor')
- grad_w_up: float32 [1024, 4096], P('dp', 'tensor')
- grad_w_down: float32 [1024, 4096], P('dp', 'tensor')
- grad_b_qkv: float32 [3072], P('tensor')
- grad_b_up: float32 [4096], P('tensor')
- grad_ln1_gain: float32 [1024], replicated
- grad_ln1_bias: float32 [1024], replicated
- grad_ln2_gain: float32 [1024], replicated
- grad_ln2_bias: float32 [1024], replicated
- grad_b_out: float32 [1024], replicated
- grad_b_down: float32 [1024], replicated
Inputs may be any that keep to these rules, and one draw needn't show every extreme that they name: `lengths`: live tokens of each sequence, at its start; keys from the length on are padding; some sequence has all 1024 live. `block_ids`: along each sequence the block number starts at 0 and never falls; each block spans 1 to 256 consecutive positions and some block spans exactly 256.
All inputs are finite; a program needn't handle non-finite values.
Results may differ from a plain program's by a relative error of at most 0.0098.
Values may be sent and summed in bfloat16 or wider, within the bound.
A program may use at most 256 MiB of HBM per device.

v0:
```python
import jax
import jax.numpy as jnp
from jax import lax
from jax.sharding import PartitionSpec as P

HEAD = 64
ROT = 16
BLOCK = 256
MICRO = 2


def layer_norm(values, ln_gain, ln_bias):
    centre = jnp.mean(values, axis=-1, keepdims=True)
    shifted = values - centre
    spread = jnp.mean(shifted * shifted, axis=-1, keepdims=True)
    return shifted * lax.rsqrt(spread + 1e-05) * ln_gain + ln_bias


def rope_tables(length, rotary):
    halved = rotary // 2
    frequency = 1.0 / 10000.0 ** (jnp.arange(halved, dtype=jnp.float32) * (2.0 / rotary))
    angles = jnp.arange(length, dtype=jnp.float32)[:, None] * frequency[None, :]
    angles = jnp.concatenate([angles, angles], axis=1)[:, None, :]
    return (jnp.cos(angles), jnp.sin(angles))


def rotate(head_rows, cos_table, sin_table, rotary):
    halved = rotary // 2
    moving = head_rows[..., :rotary]
    turned = jnp.concatenate([-moving[..., halved:], moving[..., :halved]], axis=-1)
    moving = moving * cos_table + turned * sin_table
    return jnp.concatenate([moving, head_rows[..., rotary:]], axis=-1)


def visible(block_rows, limits, first_row, tile_rows, key_end):
    own_ids = block_rows[:, first_row : first_row + tile_rows]
    key_pos = jnp.arange(key_end, dtype=jnp.int32)
    allowed = (block_rows[:, None, :key_end] <= own_ids[:, :, None]) & (
        key_pos[None, None, :] < limits[:, None, None]
    )
    return allowed[:, None]


def gelu_exact(argument):
    return jax.nn.gelu(argument, approximate=False)


def on_device(
    inputs,
    cotangent,
    lengths,
    block_ids,
    ln1_gain,
    ln1_bias,
    ln2_gain,
    ln2_bias,
    w_qkv,
    b_qkv,
    w_out,
    b_out,
    w_up,
    b_up,
    w_down,
    b_down,
):
    model_width = inputs.shape[2]
    per_micro = inputs.shape[0] // MICRO
    length = block_ids.shape[1]
    tile_rows = min(512, length)
    heads_here = w_qkv.shape[1] // (3 * HEAD)
    scaling = HEAD ** (-0.5)
    cos_table, sin_table = rope_tables(length, ROT)
    grad_qkv = jnp.zeros((model_width, w_qkv.shape[1]), jnp.float32)
    grad_outw = jnp.zeros((model_width, w_out.shape[1]), jnp.float32)
    grad_upw = jnp.zeros((model_width, w_up.shape[1]), jnp.float32)
    grad_downw = jnp.zeros((model_width, w_down.shape[1]), jnp.float32)
    sum_bias_qkv = jnp.zeros((w_qkv.shape[1],), jnp.float32)
    sum_bias_up = jnp.zeros((w_up.shape[1],), jnp.float32)
    sum_gain_one = jnp.zeros((model_width,), jnp.float32)
    sum_bias_one = jnp.zeros((model_width,), jnp.float32)
    sum_gain_two = jnp.zeros((model_width,), jnp.float32)
    sum_bias_two = jnp.zeros((model_width,), jnp.float32)
    sum_slope = jnp.zeros((model_width,), jnp.float32)
    out_rows = []
    grad_rows = []
    tile_starts = list(range(0, length, tile_rows))
    key_ends = [min(length, first_row + tile_rows + BLOCK) for first_row in tile_starts]
    for micro_idx in range(MICRO):
        first_seq = micro_idx * per_micro
        last_seq = first_seq + per_micro
        residual = inputs[first_seq:last_seq].astype(jnp.float32)
        limits = lengths[first_seq:last_seq]
        block_rows = block_ids[first_seq:last_seq]
        value_one, norm_one_back = jax.vjp(layer_norm, residual, ln1_gain, ln1_bias)
        value_two, norm_two_back = jax.vjp(layer_norm, residual, ln2_gain, ln2_bias)
        whole_one, whole_two = (
            lax.all_gather(value_one.astype(jnp.bfloat16), "tensor", axis=1, tiled=True),
            lax.all_gather(value_two.astype(jnp.bfloat16), "tensor", axis=1, tiled=True),
        )
        qkv_full, out_full, up_full, down_full = (
            lax.all_gather(w_qkv, "dp", axis=0, tiled=True),
            lax.all_gather(w_out, "dp", axis=0, tiled=True),
            lax.all_gather(w_up, "dp", axis=0, tiled=True),
            lax.all_gather(w_down, "dp", axis=0, tiled=True),
        )
        projected = (
            jnp.einsum("bsd,dc->bsc", whole_one, qkv_full, preferred_element_type=jnp.float32)
            + b_qkv
        )
        projected = projected.reshape(per_micro, length, heads_here, 3, HEAD)
        queries = rotate(projected[:, :, :, 0], cos_table, sin_table, ROT).astype(jnp.bfloat16)
        key_rows = rotate(projected[:, :, :, 1], cos_table, sin_table, ROT).astype(jnp.bfloat16)
        values = projected[:, :, :, 2].astype(jnp.bfloat16)
        scaled_q = (queries * jnp.bfloat16(scaling)).transpose(0, 2, 1, 3)
        keys_hd = key_rows.transpose(0, 2, 1, 3)
        values_hd = values.transpose(0, 2, 1, 3)
        log_sums = []
        mixed_parts = []
        for first_row, key_end in zip(tile_starts, key_ends):
            q_block = scaled_q[:, :, first_row : first_row + tile_rows]
            allowed = visible(block_rows, limits, first_row, tile_rows, key_end)
            scores = jnp.einsum(
                "bhqe,bhke->bhqk",
                q_block,
                keys_hd[:, :, :key_end],
                preferred_element_type=jnp.float32,
            )
            scores = jnp.where(allowed, scores, -1e30)
            row_peak = jnp.max(scores, axis=-1)
            powered = jnp.exp(scores - row_peak[..., None])
            totals = jnp.sum(powered, axis=-1)
            soft_low = (powered / totals[..., None]).astype(jnp.bfloat16)
            log_sums.append(row_peak + jnp.log(totals))
            mixed_parts.append(
                jnp.einsum(
                    "bhqk,bhke->bhqe",
                    soft_low,
                    values_hd[:, :, :key_end],
                    preferred_element_type=jnp.float32,
                )
            )
        attended = (
            jnp.concatenate(mixed_parts, axis=2)
            .transpose(0, 2, 1, 3)
            .reshape(per_micro, length, heads_here * HEAD)
            .astype(jnp.bfloat16)
        )
        partial_sum = jnp.einsum(
            "bsf,df->bsd", attended, out_full, preferred_element_type=jnp.float32
        )
        hidden_pre = (
            jnp.einsum("bsd,df->bsf", whole_two, up_full, preferred_element_type=jnp.float32) + b_up
        )
        gelu_value, gelu_back = jax.vjp(gelu_exact, hidden_pre)
        activated = gelu_value.astype(jnp.bfloat16)
        partial_sum = partial_sum + jnp.einsum(
            "bsf,df->bsd", activated, down_full, preferred_element_type=jnp.float32
        )
        reduced = lax.psum_scatter(partial_sum, "tensor", scatter_dimension=1, tiled=True)
        out_rows.append((residual + reduced + b_out + b_down).astype(jnp.bfloat16))
        slope_local = cotangent[first_seq:last_seq]
        slope = lax.all_gather(slope_local, "tensor", axis=1, tiled=True)
        qkv_full, out_full, up_full, down_full = (
            lax.all_gather(w_qkv, "dp", axis=0, tiled=True),
            lax.all_gather(w_out, "dp", axis=0, tiled=True),
            lax.all_gather(w_up, "dp", axis=0, tiled=True),
            lax.all_gather(w_down, "dp", axis=0, tiled=True),
        )
        grad_outw = grad_outw + jnp.einsum(
            "bsd,bsf->df", slope, attended, preferred_element_type=jnp.float32
        )
        grad_downw = grad_downw + jnp.einsum(
            "bsd,bsf->df", slope, activated, preferred_element_type=jnp.float32
        )
        grad_att = jnp.einsum(
            "bsd,df->bsf", slope, out_full, preferred_element_type=jnp.float32
        ).astype(jnp.bfloat16)
        grad_att = grad_att.reshape(per_micro, length, heads_here, HEAD).transpose(0, 2, 1, 3)
        grad_act = jnp.einsum("bsd,df->bsf", slope, down_full, preferred_element_type=jnp.float32)
        grad_hidden = gelu_back(grad_act)[0].astype(jnp.bfloat16)
        grad_upw = grad_upw + jnp.einsum(
            "bsd,bsf->df", whole_two, grad_hidden, preferred_element_type=jnp.float32
        )
        sum_bias_up = sum_bias_up + jnp.sum(grad_hidden.astype(jnp.float32), axis=(0, 1))
        grad_two = jnp.einsum(
            "bsf,df->bsd", grad_hidden, up_full, preferred_element_type=jnp.float32
        )
        grad_keys = jnp.zeros((per_micro, heads_here, length, HEAD), jnp.float32)
        grad_values = jnp.zeros((per_micro, heads_here, length, HEAD), jnp.float32)
        query_parts = []
        for index_tile, first_row in enumerate(tile_starts):
            key_end = key_ends[index_tile]
            q_block = scaled_q[:, :, first_row : first_row + tile_rows]
            g_block = grad_att[:, :, first_row : first_row + tile_rows]
            k_block = keys_hd[:, :, :key_end]
            allowed = visible(block_rows, limits, first_row, tile_rows, key_end)
            scores = jnp.einsum(
                "bhqe,bhke->bhqk", q_block, k_block, preferred_element_type=jnp.float32
            )
            scores = jnp.where(allowed, scores, -1e30)
            soft_full = jnp.exp(scores - log_sums[index_tile][..., None])
            soft_low = soft_full.astype(jnp.bfloat16)
            value_part = jnp.einsum(
                "bhqk,bhqe->bhke", soft_low, g_block, preferred_element_type=jnp.float32
            )
            grad_values = grad_values.at[:, :, :key_end].add(value_part)
            grad_soft = jnp.einsum(
                "bhqe,bhke->bhqk",
                g_block,
                values_hd[:, :, :key_end],
                preferred_element_type=jnp.float32,
            )
            centred = jnp.sum(soft_full * grad_soft, axis=-1)
            grad_scores = (soft_full * (grad_soft - centred[..., None])).astype(jnp.bfloat16)
            query_parts.append(
                jnp.einsum(
                    "bhqk,bhke->bhqe", grad_scores, k_block, preferred_element_type=jnp.float32
                )
                * scaling
            )
            key_part = jnp.einsum(
                "bhqk,bhqe->bhke", grad_scores, q_block, preferred_element_type=jnp.float32
            )
            grad_keys = grad_keys.at[:, :, :key_end].add(key_part)
        grad_queries = jnp.concatenate(query_parts, axis=2).transpose(0, 2, 1, 3)
        grad_keys = grad_keys.transpose(0, 2, 1, 3)
        grad_values = grad_values.transpose(0, 2, 1, 3)
        grad_projected = jnp.stack(
            [
                rotate(grad_queries, cos_table, -sin_table, ROT),
                rotate(grad_keys, cos_table, -sin_table, ROT),
                grad_values,
            ],
            axis=3,
        )
        grad_projected = grad_projected.reshape(per_micro, length, 3 * heads_here * HEAD).astype(
            jnp.bfloat16
        )
        grad_qkv = grad_qkv + jnp.einsum(
            "bsd,bsc->dc", whole_one, grad_projected, preferred_element_type=jnp.float32
        )
        sum_bias_qkv = sum_bias_qkv + jnp.sum(grad_projected.astype(jnp.float32), axis=(0, 1))
        grad_one = jnp.einsum(
            "bsc,dc->bsd", grad_projected, qkv_full, preferred_element_type=jnp.float32
        )
        slope_rows = slope_local.astype(jnp.float32)
        back_one, back_two = (
            lax.psum_scatter(grad_one, "tensor", scatter_dimension=1, tiled=True),
            lax.psum_scatter(grad_two, "tensor", scatter_dimension=1, tiled=True),
        )
        input_one, gain_one, bias_one = norm_one_back(back_one)
        input_two, gain_two, bias_two = norm_two_back(back_two)
        grad_rows.append(slope_rows + input_one + input_two)
        sum_gain_one = sum_gain_one + gain_one
        sum_bias_one = sum_bias_one + bias_one
        sum_gain_two = sum_gain_two + gain_two
        sum_bias_two = sum_bias_two + bias_two
        sum_slope = sum_slope + jnp.sum(slope_rows, axis=(0, 1))
    reduced_grads = (
        lax.psum_scatter(grad_qkv, "dp", scatter_dimension=0, tiled=True),
        lax.psum_scatter(grad_outw, "dp", scatter_dimension=0, tiled=True),
        lax.psum_scatter(grad_upw, "dp", scatter_dimension=0, tiled=True),
        lax.psum_scatter(grad_downw, "dp", scatter_dimension=0, tiled=True),
    )
    bias_qkv_total, bias_up_total = lax.psum((sum_bias_qkv, sum_bias_up), "dp")
    shared = lax.psum(
        (sum_gain_one, sum_bias_one, sum_gain_two, sum_bias_two, sum_slope), ("dp", "tensor")
    )
    return (
        jnp.concatenate(out_rows, axis=0),
        jnp.concatenate(grad_rows, axis=0),
        reduced_grads[0],
        reduced_grads[1],
        reduced_grads[2],
        reduced_grads[3],
        bias_qkv_total,
        bias_up_total,
        shared[0],
        shared[1],
        shared[2],
        shared[3],
        shared[4],
        shared[4],
    )


def solution(mesh):
    in_specs = (
        P("dp", "tensor", None),
        P("dp", "tensor", None),
        P("dp"),
        P("dp", None),
        P(),
        P(),
        P(),
        P(),
        P("dp", "tensor"),
        P("tensor"),
        P("dp", "tensor"),
        P(),
        P("dp", "tensor"),
        P("tensor"),
        P("dp", "tensor"),
        P(),
    )
    out_specs = (
        P("dp", "tensor", None),
        P("dp", "tensor", None),
        P("dp", "tensor"),
        P("dp", "tensor"),
        P("dp", "tensor"),
        P("dp", "tensor"),
        P("tensor"),
        P("tensor"),
        P(),
        P(),
        P(),
        P(),
        P(),
        P(),
    )
    return jax.shard_map(
        on_device, mesh=mesh, in_specs=in_specs, out_specs=out_specs, check_vma=False
    )
```

profile of v0, /device:TPU:0, one launch (start us, length us, event | category | flops | bytes accessed | tf_op | source)
XLA Modules:
  0.0 1063.5 jit_solution(9621609152329100266)
XLA Ops:
  24.5 12.7 %all_gather.44 = bf16[1024,256]{1,0:T(8,128)(2,1)S(1)} all-gather(bf16[128,256]{1,0:T(8,128)(2,1)S(1)} %copy-done.88), channel_id=1, replica_groups=mesh['dp'=8,'tensor'=4] {'dp'}, dimensions={0}, use_global_device_ids=true | all-gather | bytes 589824 | tf_op jit(solution)/shard_map/all_gather | solution.py:102
  39.7 48.1 %all-gather.10.cloned.1.call-done = bf16[1,1024,1024]{2,1,0:T(8,128)(2,1)} async-done(((bf16[1,256,1024]{2,1,0:T(8,128)(2,1)}), bf16[1,1024,1024]{2,1,0:T(8,128)(2,1)}) %all-gather.10.cloned.1.call-update) | async-done | bytes 2097168 | tf_op jit(solution)/shard_map/all_gather | solution.py:97
  96.9 37.2 %all-gather.20.cloned.1.call-done = bf16[1,1024,1024]{2,1,0:T(8,128)(2,1)} async-done(((bf16[1,256,1024]{2,1,0:T(8,128)(2,1)}), bf16[1,1024,1024]{2,1,0:T(8,128)(2,1)}) %all-gather.20.cloned.1.call-update) | async-done | bytes 2097168 | tf_op jit(solution)/shard_map/all_gather | solution.py:97
  150.5 29.7 %all-gather.24.cloned.1.call-done = bf16[1,1024,1024]{2,1,0:T(8,128)(2,1)} async-done(((bf16[1,256,1024]{2,1,0:T(8,128)(2,1)}), bf16[1,1024,1024]{2,1,0:T(8,128)(2,1)}) %all-gather.24.cloned.1.call-update) | async-done | bytes 2097168 | tf_op jit(solution)/shard_map/all_gather | solution.py:162
  182.6 4.8 multiply_reduce_fusion.3
  215.9 10.4 all-gather.26.cloned.1.call-done
  234.4 6.3 multiply_reduce_fusion.1
  251.7 21.3 %all-gather.22.cloned.1.call-done = bf16[1,1024,1024]{2,1,0:T(8,128)(2,1)} async-done(((bf16[1,256,1024]{2,1,0:T(8,128)(2,1)}), bf16[1,1024,1024]{2,1,0:T(8,128)(2,1)}) %all-gather.22.cloned.1.call-update) | async-done | bytes 2097168 | tf_op jit(solution)/shard_map/all_gather | solution.py:98
  273.0 28.5 %all-gather.16.cloned.1.call-done = bf16[1024,1024]{1,0:T(8,128)(2,1)} async-done(((bf16[128,1024]{1,0:T(8,128)(2,1)}), bf16[1024,1024]{1,0:T(8,128)(2,1)}) %all-gather.16.cloned.1.call-update) | async-done | bytes 2097168 | tf_op jit(solution)/shard_map/all_gather | solution.py:103
  301.5 6.6 fusion.66
  308.2 41.5 %all-gather.14.cloned.1.call-done = bf16[1,1024,1024]{2,1,0:T(8,128)(2,1)} async-done(((bf16[1,256,1024]{2,1,0:T(8,128)(2,1)}), bf16[1,1024,1024]{2,1,0:T(8,128)(2,1)}) %all-gather.14.cloned.1.call-update) | async-done | bytes 2097168 | tf_op jit(solution)/shard_map/all_gather | solution.py:98
  349.6 23.9 %multiply_convert_fusion.5 = (bf16[1024,1024]{1,0:T(8,128)(2,1)S(1)}, f32[1024,1024]{1,0:T(8,128)}, bf16[1024,1024]{1,0:T(8,128)(2,1)S(1)}, f32[1024,1024]{1,0:T(8,128)}, f32[1024,1024]{1,0:T(8,128)}) fusion(f32[1024]{0:T(1024)} %param.53, f32[1024,1024]{1,0:T(8,128)} %fusion.66, bf16[1024,1024]{1,0:T(8,128)(2,1)} %all-gather.16.cloned.1.call-done, ...), kind=kOutput, calls=%fused_computation.58 | convolution fusion | flops 2285895680 | bytes 25169920 | tf_op jit(solution)/shard_map/bsd,df->bsf/dot_general | solution.py:152
  376.7 4.5 add_bitcast_fusion
  388.4 6.6 multiply_reduce_fusion
  414.7 4.4 fusion.151
  419.1 4.7 fusion.133
  431.1 7.4 convert_reduce_fusion
  439.9 4.4 convolution_bitcast_fusion.2
  445.9 6.8 convert_reduce_fusion.1
  454.2 4.5 convolution_bitcast_fusion.3
  482.6 4.8 fusion.64
  487.4 4.5 fusion.80
  492.2 16.0 %all-reduce.5 = (f32[768]{0:T(1024)}, f32[1024]{0:T(1024)}) all-reduce(f32[768]{0:T(1024)S(1)} %add.401, f32[1024]{0:T(1024)S(1)} %add.402), channel_id=1, replica_groups=mesh['dp'=8,'tensor'=4] {'dp'}, use_global_device_ids=true, to_apply=%region_36.37 | all-reduce | flops 1792 | bytes 14336 | tf_op jit(solution)/shard_map/psum | solution.py:265
  511.8 39.2 %reduce-scatter.15.cloned.1.call-done = f32[1,256,1024]{2,1,0:T(8,128)} async-done(((f32[1,1024,1024]{2,1,0:T(8,128)}), f32[1,256,1024]{2,1,0:T(8,128)}) %reduce-scatter.15.cloned.1.call-update) | async-done | bytes 1048592 | tf_op jit(solution)/shard_map/reduce_scatter | solution.py:248
  551.1 79.6 %reduce-scatter.19.cloned.1.call-done = f32[1,256,1024]{2,1,0:T(8,128)} async-done(((f32[1,1024,1024]{2,1,0:T(8,128)}), f32[1,256,1024]{2,1,0:T(8,128)}) %reduce-scatter.19.cloned.1.call-update) | async-done | bytes 1048592 | tf_op jit(solution)/shard_map/reduce_scatter | solution.py:248
  632.7 77.5 %reduce-scatter.21.cloned.1.call-done = f32[1,256,1024]{2,1,0:T(8,128)} async-done(((f32[1,1024,1024]{2,1,0:T(8,128)}), f32[1,256,1024]{2,1,0:T(8,128)}) %reduce-scatter.21.cloned.1.call-update) | async-done | bytes 1048592 | tf_op jit(solution)/shard_map/reduce_scatter | solution.py:249
  710.2 79.4 %reduce-scatter.17.cloned.1.call-done = f32[1,256,1024]{2,1,0:T(8,128)} async-done(((f32[1,1024,1024]{2,1,0:T(8,128)}), f32[1,256,1024]{2,1,0:T(8,128)}) %reduce-scatter.17.cloned.1.call-update) | async-done | bytes 1048592 | tf_op jit(solution)/shard_map/reduce_scatter | solution.py:249
  795.8 44.0 %all-reduce.4 = (f32[1024]{0:T(1024)}, f32[1024]{0:T(1024)}, f32[1024]{0:T(1024)}, f32[1024]{0:T(1024)}, f32[1024]{0:T(1024)S(1)}) all-reduce(f32[1024]{0:T(1024)S(1)} %add.403, f32[1024]{0:T(1024)S(1)} %add.404, f32[1024]{0:T(1024)S(1)} %add.405, f32[1024]{0:T(1024)S(1)} %add.406, ...), channel_id=1, replica_groups=mesh['dp'=8,'tensor'=4] {'dp','tensor'}, use_global_device_ids=true, to_apply=%region_42.43 | all-reduce | flops 5120 | bytes 40960 | tf_op jit(solution)/shard_map/psum | solution.py:266
  839.8 30.5 %reduce-scatter.13.cloned.1.call-done = f32[1,256,1024]{2,1,0:T(8,128)} async-done(((f32[1,1024,1024]{2,1,0:T(8,128)}), f32[1,256,1024]{2,1,0:T(8,128)}) %reduce-scatter.13.cloned.1.call-update) | async-done | bytes 1048592 | tf_op jit(solution)/shard_map/reduce_scatter | solution.py:159
  870.2 79.4 %reduce-scatter.11.cloned.1.call-done = f32[1,256,1024]{2,1,0:T(8,128)} async-done(((f32[1,1024,1024]{2,1,0:T(8,128)}), f32[1,256,1024]{2,1,0:T(8,128)}) %reduce-scatter.11.cloned.1.call-update) | async-done | bytes 1048592 | tf_op jit(solution)/shard_map/reduce_scatter | solution.py:159
  954.9 45.7 %reduce-scatter.23.cloned.1.call-done = f32[128,768]{1,0:T(8,128)} async-done(((f32[1024,768]{1,0:T(8,128)}), f32[128,768]{1,0:T(8,128)}) %reduce-scatter.23.cloned.1.call-update) | async-done | bytes 393232 | tf_op jit(solution)/shard_map/reduce_scatter | solution.py:260
  1000.6 55.3 %reduce-scatter.27.cloned.1.call-done = f32[128,1024]{1,0:T(8,128)} async-done(((f32[1024,1024]{1,0:T(8,128)}), f32[128,1024]{1,0:T(8,128)}) %reduce-scatter.27.cloned.1.call-update) | async-done | bytes 524304 | tf_op jit(solution)/shard_map/reduce_scatter | solution.py:262
  (447 shorter events, 177.0 us)
Async XLA Ops:
  7.2 32.6 %all-gather.12.cloned.1.call-start = ((), (), s32[]{:S(2)}) async-start(), calls=%async_computation.11 | async-start | bytes 1769472 | tf_op jit(solution)/shard_map/all_gather | solution.py:101
  7.9 79.9 %all-gather.10.cloned.1.call-start = ((), (), s32[]{:S(2)}) async-start(), calls=%async_computation.10 | async-start | bytes 2621440 | tf_op jit(solution)/shard_map/all_gather | solution.py:97
  14.9 119.2 %all-gather.20.cloned.1.call-start = ((), (), s32[]{:S(2)}) async-start(), calls=%async_computation.16 | async-start | bytes 2621440 | tf_op jit(solution)/shard_map/all_gather | solution.py:97
  15.6 164.6 %all-gather.24.cloned.1.call-start = ((), (), s32[]{:S(2)}) async-start(), calls=%async_computation.19 | async-start | bytes 2621440 | tf_op jit(solution)/shard_map/all_gather | solution.py:162
  16.8 209.5 %all-gather.26.cloned.1.call-start = ((), (), s32[]{:S(2)}) async-start(), calls=%async_computation.22 | async-start | bytes 2621440 | tf_op jit(solution)/shard_map/all_gather | solution.py:162
  17.4 255.6 %all-gather.22.cloned.1.call-start = ((), (), s32[]{:S(2)}) async-start(), calls=%async_computation.17 | async-start | bytes 2621440 | tf_op jit(solution)/shard_map/all_gather | solution.py:98
  18.0 283.6 %all-gather.16.cloned.1.call-start = ((), (), s32[]{:S(2)}) async-start(), calls=%async_computation.13 | async-start | bytes 2359296 | tf_op jit(solution)/shard_map/all_gather | solution.py:103
  18.7 330.9 %all-gather.14.cloned.1.call-start = ((), (), s32[]{:S(2)}) async-start(), calls=%async_computation.12 | async-start | bytes 2621440 | tf_op jit(solution)/shard_map/all_gather | solution.py:98
  19.5 410.0 %all-gather.18.cloned.1.call-start = ((), (), s32[]{:S(2)}) async-start(), calls=%async_computation.14 | async-start | bytes 2359296 | tf_op jit(solution)/shard_map/all_gather | solution.py:104
  20.2 487.9 %reduce-scatter.25.cloned.1.call-start = ((), (), s32[]{:S(2)}) async-start(), calls=%async_computation.26 | async-start | bytes 1179648 | tf_op jit(solution)/shard_map/reduce_scatter | solution.py:261
  37.2 189.1 %copy-start.21 = (bf16[1024,256]{1,0:T(8,128)(2,1)}, bf16[1024,256]{1,0:T(8,128)(2,1)S(1)}, u32[]{:S(2)}) copy-start(bf16[1024,256]{1,0:T(8,128)(2,1)S(1)} %all_gather.44) | copy-start | bytes 1572868
  37.6 173.3 %copy-start.7 = (pred[512,1024]{1,0:T(8,128)(4,1)}, pred[512,1024]{1,0:T(8,128)(4,1)S(1)}, u32[]{:S(2)}) copy-start(pred[512,1024]{1,0:T(8,128)(4,1)S(1)} %compare_and_fusion) | copy-start | bytes 1572868
  38.0 202.7 %copy-start.10 = (pred[512,1024]{1,0:T(8,128)(4,1)}, pred[512,1024]{1,0:T(8,128)(4,1)S(1)}, u32[]{:S(2)}) copy-start(pred[512,1024]{1,0:T(8,128)(4,1)S(1)} %compare_and_fusion.1) | copy-start | bytes 1572868
  38.6 148.7 %copy-start.5 = (pred[512,768]{1,0:T(8,128)(4,1)}, pred[512,768]{1,0:T(8,128)(4,1)S(1)}, u32[]{:S(2)}) copy-start(pred[512,768]{1,0:T(8,128)(4,1)S(1)} %get-tuple-element.314) | copy-start | bytes 1179652
  251.6 258.2 %reduce-scatter.29.cloned.1.call-start = ((), (), s32[]{:S(2)}) async-start(), calls=%async_computation.28 | async-start | bytes 4718592 | tf_op jit(solution)/shard_map/reduce_scatter | solution.py:263
  381.2 169.8 %reduce-scatter.15.cloned.1.call-start = ((), (), s32[]{:S(2)}) async-start(), calls=%async_computation.20 | async-start | bytes 5242880 | tf_op jit(solution)/shard_map/reduce_scatter | solution.py:248
  413.1 217.5 %reduce-scatter.19.cloned.1.call-start = ((), (), s32[]{:S(2)}) async-start(), calls=%async_computation.23 | async-start | bytes 5242880 | tf_op jit(solution)/shard_map/reduce_scatter | solution.py:248
  429.4 280.8 %reduce-scatter.21.cloned.1.call-start = ((), (), s32[]{:S(2)}) async-start(), calls=%async_computation.24 | async-start | bytes 5242880 | tf_op jit(solution)/shard_map/reduce_scatter | solution.py:249
  444.3 345.3 %reduce-scatter.17.cloned.1.call-start = ((), (), s32[]{:S(2)}) async-start(), calls=%async_computation.21 | async-start | bytes 5242880 | tf_op jit(solution)/shard_map/reduce_scatter | solution.py:249
  458.7 411.6 %reduce-scatter.13.cloned.1.call-start = ((), (), s32[]{:S(2)}) async-start(), calls=%async_computation.18 | async-start | bytes 5242880 | tf_op jit(solution)/shard_map/reduce_scatter | solution.py:159
  467.0 482.6 %reduce-scatter.11.cloned.1.call-start = ((), (), s32[]{:S(2)}) async-start(), calls=%async_computation.15 | async-start | bytes 5242880 | tf_op jit(solution)/shard_map/reduce_scatter | solution.py:159
  473.9 526.7 %reduce-scatter.23.cloned.1.call-start = ((), (), s32[]{:S(2)}) async-start(), calls=%async_computation.25 | async-start | bytes 3538944 | tf_op jit(solution)/shard_map/reduce_scatter | solution.py:260
  482.5 573.3 %reduce-scatter.27.cloned.1.call-start = ((), (), s32[]{:S(2)}) async-start(), calls=%async_computation.27 | async-start | bytes 4718592 | tf_op jit(solution)/shard_map/reduce_scatter | solution.py:262
  492.0 140.7 %copy-start.101 = (f32[256]{0:T(256)S(1)}, f32[256]{0:T(256)}, u32[]{:S(2)}) copy-start(f32[256]{0:T(256)} %copy-done.100) | copy-start | bytes 3076
  492.0 140.7 %copy-start.99 = (f32[256]{0:T(256)S(1)}, f32[256]{0:T(256)}, u32[]{:S(2)}) copy-start(f32[256]{0:T(256)} %copy-done.98) | copy-start | bytes 3076
  492.0 297.6 %copy-start.82 = (f32[1024]{0:T(1024)S(1)}, f32[1024]{0:T(1024)}, u32[]{:S(2)}) copy-start(f32[1024]{0:T(1024)} %param.46) | copy-start | bytes 12292
  492.0 297.6 %copy-start.95 = (f32[256]{0:T(256)S(1)}, f32[256]{0:T(256)}, u32[]{:S(2)}) copy-start(f32[256]{0:T(256)} %copy-done.94) | copy-start | bytes 3076
  492.0 297.6 %copy-start.97 = (f32[256]{0:T(256)S(1)}, f32[256]{0:T(256)}, u32[]{:S(2)}) copy-start(f32[256]{0:T(256)} %copy-done.96) | copy-start | bytes 3076
  792.9 156.7 %copy-start.13 = (f32[1,256,1024]{2,1,0:T(8,128)S(1)}, f32[1,256,1024]{2,1,0:T(8,128)}, u32[]{:S(2)}) copy-start(f32[1,256,1024]{2,1,0:T(8,128)} %reduce-scatter.19.cloned.1.call-done) | copy-start | bytes 3145732
  792.9 156.7 %copy-start.102 = (f32[1024]{0:T(1024)S(1)}, f32[1024]{0:T(1024)}, u32[]{:S(2)}) copy-start(f32[1024]{0:T(1024)} %param.55) | copy-start | bytes 12292
  792.9 156.7 %copy-start.103 = (f32[1024]{0:T(1024)S(1)}, f32[1024]{0:T(1024)}, u32[]{:S(2)}) copy-start(f32[1024]{0:T(1024)} %param.51) | copy-start | bytes 12292
  839.7 216.1 %copy-start.104 = (f32[1024]{0:T(1024)}, f32[1024]{0:T(1024)S(1)}, u32[]{:S(2)}) copy-start(f32[1024]{0:T(1024)S(1)} %get-tuple-element.342) | copy-start | bytes 12292
  (119 other events, 1309.8 us)
Sparse Core Ops, SparseCore 0:
  9.9 29.7 all-gather.11
  41.9 45.9 all-gather.9
  89.4 44.6 all-gather.19
  135.5 44.6 all-gather.23
  181.6 44.6 all-gather.25
  228.3 44.6 all-gather.21
  274.9 26.5 all-gather.15
  303.7 45.9 all-gather.13
  351.5 26.6 all-gather.17
  381.2 36.0 reduce-scatter.24
  420.7 51.3 reduce-scatter.28
  474.3 76.7 reduce-scatter.14
  553.4 77.2 reduce-scatter.18
  632.9 77.2 reduce-scatter.20
  712.3 77.2 reduce-scatter.16
  791.9 78.3 reduce-scatter.12
  872.4 77.2 reduce-scatter.10
  953.8 46.7 reduce-scatter.22
  1004.5 51.2 reduce-scatter.26
where the time goes:
time: 1070 us; the launch traced here: 1060 us
  waiting for transfers between devices  709 us (66%)
  matrix products  181 us (17%)
  blocking collectives  72.7 us (7%)
  other arithmetic  48.3 us (5%)
  local copies, waits for them, and re-layouts  35.3 us (3%)
  between operations  16.4 us (2%)
    reduce_scatter x2, waiting for transfers between devices, on_device(): lax.psum_scatter(grad_two, 'tensor', scatter_dimension=1, tiled=True)  157 us
    reduce_scatter x2, waiting for transfers between devices, on_device(): lax.psum_scatter(grad_one, 'tensor', scatter_dimension=1, tiled=True)  119 us
    reduce_scatter x2, waiting for transfers between devices, on_device(): lax.psum_scatter(partial_sum, 'tensor', scatter_dimension=1, tiled=True)  110 us
    all_gather x2, waiting for transfers between devices, on_device(): lax.all_gather(value_one.astype(jnp.bfloat16), 'tensor', axis=1, tiled=True)  85.3 us
    all_gather x2, waiting for transfers between devices, on_device(): lax.all_gather(value_two.astype(jnp.bfloat16), 'tensor', axis=1, tiled=True)  62.8 us
    reduce_scatter x1, waiting for transfers between devices, on_device(): lax.psum_scatter(grad_upw, 'dp', scatter_dimension=0, tiled=True)  55.3 us
    reduce_scatter x1, waiting for transfers between devices, on_device(): lax.psum_scatter(grad_qkv, 'dp', scatter_dimension=0, tiled=True)  45.7 us
    psum x1, blocking collectives, on_device(): lax.psum((sum_gain_one, sum_bias_one, sum_gain_two, sum_bias_two, sum_slo...  44 us
  transfers between devices with their start and end apart: 19, of which 16 were waited for; matrix products, arithmetic and copies ran while one was open for 23% of the time, Pallas kernels for 0%

commit v1 on v0

--- a/solution.py
+++ b/solution.py
@@ -7,6 +7,18 @@
 ROT = 16
 BLOCK = 256
 MICRO = 2
+
+
+def doubled_up(array, axis, dim):
+    ways, here = (lax.axis_size(axis), lax.axis_index(axis))
+    grown, reach = (array, 1)
+    while reach < ways:
+        theirs = lax.ppermute(grown, axis, [(d, d ^ reach) for d in range(ways)])
+        mine_first = jnp.concatenate([grown, theirs], axis=dim)
+        theirs_first = jnp.concatenate([theirs, grown], axis=dim)
+        grown = jnp.where(here & reach == 0, mine_first, theirs_first)
+        reach = 2 * reach
+    return grown
 
 
 def layer_norm(values, ln_gain, ln_bias):
@@ -100,7 +112,7 @@
         qkv_full, out_full, up_full, down_full = (
             lax.all_gather(w_qkv, "dp", axis=0, tiled=True),
             lax.all_gather(w_out, "dp", axis=0, tiled=True),
-            lax.all_gather(w_up, "dp", axis=0, tiled=True),
+            doubled_up(w_up, "dp", 0),
             lax.all_gather(w_down, "dp", axis=0, tiled=True),
         )
         projected = (

time: 1070 us -> 1070 us (level)
  waiting for transfers between devices: 709 us -> 692 us
    all_gather x1, waiting for transfers between devices: 28.5 us -> 0.01 us  [on_device(): lax.all_gather(w_up, 'dp', axis=0, tiled=True)]
    reduce_scatter x2, waiting for transfers between devices: 119 us -> 143 us  [on_device(): lax.psum_scatter(grad_one, 'tensor', scatter_dimension=1, tiled=True)]
    all_gather x2, waiting for transfers between devices: 85.3 us -> 70.2 us  [on_device(): lax.all_gather(value_one.astype(jnp.bfloat16), 'tensor', axis=1, tiled=True)]
    ppermute x0 -> x3, waiting for transfers between devices: none -> 10.9 us  [doubled_up(): theirs = lax.ppermute(grown, axis, [(d, d ^ reach) for d in range(ways)])]
    unnamed x267 -> x291, local copies, waits for them, and re-layouts: 23.3 us -> 26.5 us
  transfers between devices with their start and end apart: 19 -> 22, of which waited for: 16 -> 15; matrix products, arithmetic and copies ran while one was open for 23% -> 24% of each run, Pallas kernels for 0% -> 0%
where the time goes in v1:
time: 1070 us; the launch traced here: 1060 us
  waiting for transfers between devices  692 us (65%)
  matrix products  189 us (18%)
  blocking collectives  71.5 us (7%)
  other arithmetic  52.7 us (5%)
  local copies, waits for them, and re-layouts  36 us (3%)
  between operations  16.6 us (2%)
    reduce_scatter x2, waiting for transfers between devices, on_device(): lax.psum_scatter(grad_two, 'tensor', scatter_dimension=1, tiled=True)  157 us
    reduce_scatter x2, waiting for transfers between devices, on_device(): lax.psum_scatter(grad_one, 'tensor', scatter_dimension=1, tiled=True)  143 us
    reduce_scatter x2, waiting for transfers between devices, on_device(): lax.psum_scatter(partial_sum, 'tensor', scatter_dimension=1, tiled=True)  110 us
    all_gather x2, waiting for transfers between devices, on_device(): lax.all_gather(value_one.astype(jnp.bfloat16), 'tensor', axis=1, tiled=True)  70.2 us
    reduce_scatter x1, waiting for transfers between devices, on_device(): lax.psum_scatter(grad_upw, 'dp', scatter_dimension=0, tiled=True)  55.3 us
    all_gather x2, waiting for transfers between devices, on_device(): lax.all_gather(value_two.astype(jnp.bfloat16), 'tensor', axis=1, tiled=True)  54.4 us
    reduce_scatter x1, waiting for transfers between devices, on_device(): lax.psum_scatter(grad_qkv, 'dp', scatter_dimension=0, tiled=True)  45.7 us
    psum x1, blocking collectives, on_device(): lax.psum((sum_gain_one, sum_bias_one, sum_gain_two, sum_bias_two, sum_slo...  43.9 us
  transfers between devices with their start and end apart: 22, of which 15 were waited for; matrix products, arithmetic and copies ran while one was open for 24% of the time, Pallas kernels for 0%

profile of v1, /device:TPU:0, one launch (start us, length us, event | category | flops | bytes accessed | tf_op | source)
XLA Modules:
  0.0 1062.8 jit_solution(9862540360306366833)
XLA Ops:
  23.1 12.5 %all_gather.42 = bf16[1024,256]{1,0:T(8,128)(2,1)S(1)} all-gather(bf16[128,256]{1,0:T(8,128)(2,1)S(1)} %copy-done.93), channel_id=1, replica_groups=mesh['dp'=8,'tensor'=4] {'dp'}, dimensions={0}, use_global_device_ids=true | all-gather | bytes 589824 | tf_op jit(solution)/shard_map/all_gather | solution.py:114
  40.2 10.9 %collective-permute-done.1 = bf16[256,1024]{1,0:T(8,128)(2,1)S(1)} collective-permute-done((bf16[256,1024]{1,0:T(8,128)(2,1)S(1)}, bf16[256,1024]{1,0:T(8,128)(2,1)S(1)}, u32[]{:S(2)}, u32[]{:S(2)}) %collective-permute-start.1) | collective-permute-done | bytes 524320 | tf_op jit(solution)/shard_map/ppermute | solution.py:16
  54.1 33.0 %all-gather.10.cloned.1.call-done = bf16[1,1024,1024]{2,1,0:T(8,128)(2,1)} async-done(((bf16[1,256,1024]{2,1,0:T(8,128)(2,1)}), bf16[1,1024,1024]{2,1,0:T(8,128)(2,1)}) %all-gather.10.cloned.1.call-update) | async-done | bytes 2097168 | tf_op jit(solution)/shard_map/all_gather | solution.py:109
  96.3 37.2 %all-gather.18.cloned.1.call-done = bf16[1,1024,1024]{2,1,0:T(8,128)(2,1)} async-done(((bf16[1,256,1024]{2,1,0:T(8,128)(2,1)}), bf16[1,1024,1024]{2,1,0:T(8,128)(2,1)}) %all-gather.18.cloned.1.call-update) | async-done | bytes 2097168 | tf_op jit(solution)/shard_map/all_gather | solution.py:109
  171.1 8.4 all-gather.22.cloned.1.call-done
  181.9 4.7 multiply_reduce_fusion.3
  192.5 33.1 %all-gather.26.cloned.1.call-done = bf16[1,1024,1024]{2,1,0:T(8,128)(2,1)} async-done(((bf16[1,256,1024]{2,1,0:T(8,128)(2,1)}), bf16[1,1024,1024]{2,1,0:T(8,128)(2,1)}) %all-gather.26.cloned.1.call-update) | async-done | bytes 2097168 | tf_op jit(solution)/shard_map/all_gather | solution.py:174
  229.8 6.9 multiply_reduce_fusion.1
  236.7 4.6 multiply_convert_fusion.1
  252.5 4.8 multiply_reduce_fusion.2
  257.4 15.0 %all-gather.20.cloned.1.call-done = bf16[1,1024,1024]{2,1,0:T(8,128)(2,1)} async-done(((bf16[1,256,1024]{2,1,0:T(8,128)(2,1)}), bf16[1,1024,1024]{2,1,0:T(8,128)(2,1)}) %all-gather.20.cloned.1.call-update) | async-done | bytes 2097168 | tf_op jit(solution)/shard_map/all_gather | solution.py:110
  272.3 7.4 fusion.66
  279.7 39.4 %all-gather.14.cloned.1.call-done = bf16[1,1024,1024]{2,1,0:T(8,128)(2,1)} async-done(((bf16[1,256,1024]{2,1,0:T(8,128)(2,1)}), bf16[1,1024,1024]{2,1,0:T(8,128)(2,1)}) %all-gather.14.cloned.1.call-update) | async-done | bytes 2097168 | tf_op jit(solution)/shard_map/all_gather | solution.py:110
  319.1 24.1 %multiply_convert_fusion.5 = (bf16[1024,1024]{1,0:T(8,128)(2,1)S(1)}, f32[1024,1024]{1,0:T(8,128)}, bf16[1024,1024]{1,0:T(8,128)(2,1)S(1)}, f32[1024,1024]{1,0:T(8,128)}, f32[1024,1024]{1,0:T(8,128)}) fusion(f32[1024]{0:T(1024)S(1)} %copy-done.126, f32[1024,1024]{1,0:T(8,128)} %fusion.66, bf16[512,1024]{1,0:T(8,128)(2,1)} %collective-permute-done.2, ...), kind=kOutput, calls=%fused_computation.58 | convolution fusion | flops 2295332864 | bytes 25169920 | tf_op jit(solution)/shard_map/bsd,df->bsf/dot_general | solution.py:164
  351.6 4.5 add_bitcast_fusion
  363.4 5.9 multiply_reduce_fusion
  388.9 4.5 fusion.151
  393.4 4.7 fusion.133
  405.2 7.7 convert_reduce_fusion
  412.9 6.6 convolution_bitcast_fusion.2
  421.1 6.8 convert_reduce_fusion.1
  458.0 4.8 fusion.64
  468.1 15.1 %all-reduce.5 = (f32[768]{0:T(1024)}, f32[1024]{0:T(1024)}) all-reduce(f32[768]{0:T(1024)S(1)} %add.401, f32[1024]{0:T(1024)S(1)} %add.402), channel_id=1, replica_groups=mesh['dp'=8,'tensor'=4] {'dp'}, use_global_device_ids=true, to_apply=%region_36.37 | all-reduce | flops 1792 | bytes 14336 | tf_op jit(solution)/shard_map/psum | solution.py:277
  486.9 63.6 %reduce-scatter.15.cloned.1.call-done = f32[1,256,1024]{2,1,0:T(8,128)} async-done(((f32[1,1024,1024]{2,1,0:T(8,128)}), f32[1,256,1024]{2,1,0:T(8,128)}) %reduce-scatter.15.cloned.1.call-update) | async-done | bytes 1048592 | tf_op jit(solution)/shard_map/reduce_scatter | solution.py:260
  550.4 79.6 %reduce-scatter.19.cloned.1.call-done = f32[1,256,1024]{2,1,0:T(8,128)} async-done(((f32[1,1024,1024]{2,1,0:T(8,128)}), f32[1,256,1024]{2,1,0:T(8,128)}) %reduce-scatter.19.cloned.1.call-update) | async-done | bytes 1048592 | tf_op jit(solution)/shard_map/reduce_scatter | solution.py:260
  632.1 77.5 %reduce-scatter.21.cloned.1.call-done = f32[1,256,1024]{2,1,0:T(8,128)} async-done(((f32[1,1024,1024]{2,1,0:T(8,128)}), f32[1,256,1024]{2,1,0:T(8,128)}) %reduce-scatter.21.cloned.1.call-update) | async-done | bytes 1048592 | tf_op jit(solution)/shard_map/reduce_scatter | solution.py:261
  709.6 79.4 %reduce-scatter.17.cloned.1.call-done = f32[1,256,1024]{2,1,0:T(8,128)} async-done(((f32[1,1024,1024]{2,1,0:T(8,128)}), f32[1,256,1024]{2,1,0:T(8,128)}) %reduce-scatter.17.cloned.1.call-update) | async-done | bytes 1048592 | tf_op jit(solution)/shard_map/reduce_scatter | solution.py:261
  795.1 43.9 %all-reduce.4 = (f32[1024]{0:T(1024)}, f32[1024]{0:T(1024)}, f32[1024]{0:T(1024)}, f32[1024]{0:T(1024)}, f32[1024]{0:T(1024)S(1)}) all-reduce(f32[1024]{0:T(1024)S(1)} %add.403, f32[1024]{0:T(1024)S(1)} %add.404, f32[1024]{0:T(1024)S(1)} %add.405, f32[1024]{0:T(1024)S(1)} %add.406, ...), channel_id=1, replica_groups=mesh['dp'=8,'tensor'=4] {'dp','tensor'}, use_global_device_ids=true, to_apply=%region_42.43 | all-reduce | flops 5120 | bytes 40960 | tf_op jit(solution)/shard_map/psum | solution.py:278
  839.1 30.5 %reduce-scatter.13.cloned.1.call-done = f32[1,256,1024]{2,1,0:T(8,128)} async-done(((f32[1,1024,1024]{2,1,0:T(8,128)}), f32[1,256,1024]{2,1,0:T(8,128)}) %reduce-scatter.13.cloned.1.call-update) | async-done | bytes 1048592 | tf_op jit(solution)/shard_map/reduce_scatter | solution.py:171
  869.6 79.4 %reduce-scatter.11.cloned.1.call-done = f32[1,256,1024]{2,1,0:T(8,128)} async-done(((f32[1,1024,1024]{2,1,0:T(8,128)}), f32[1,256,1024]{2,1,0:T(8,128)}) %reduce-scatter.11.cloned.1.call-update) | async-done | bytes 1048592 | tf_op jit(solution)/shard_map/reduce_scatter | solution.py:171
  954.2 45.7 %reduce-scatter.23.cloned.1.call-done = f32[128,768]{1,0:T(8,128)} async-done(((f32[1024,768]{1,0:T(8,128)}), f32[128,768]{1,0:T(8,128)}) %reduce-scatter.23.cloned.1.call-update) | async-done | bytes 393232 | tf_op jit(solution)/shard_map/reduce_scatter | solution.py:272
  999.9 55.3 %reduce-scatter.27.cloned.1.call-done = f32[128,1024]{1,0:T(8,128)} async-done(((f32[1024,1024]{1,0:T(8,128)}), f32[128,1024]{1,0:T(8,128)}) %reduce-scatter.27.cloned.1.call-update) | async-done | bytes 524304 | tf_op jit(solution)/shard_map/reduce_scatter | solution.py:274
  (479 shorter events, 188.6 us)
Async XLA Ops:
  7.2 46.9 %all-gather.12.cloned.1.call-start = ((), (), s32[]{:S(2)}) async-start(), calls=%async_computation.11 | async-start | bytes 1769472 | tf_op jit(solution)/shard_map/all_gather | solution.py:113
  7.9 79.2 %all-gather.10.cloned.1.call-start = ((), (), s32[]{:S(2)}) async-start(), calls=%async_computation.10 | async-start | bytes 2621440 | tf_op jit(solution)/shard_map/all_gather | solution.py:109
  14.9 118.5 %all-gather.18.cloned.1.call-start = ((), (), s32[]{:S(2)}) async-start(), calls=%async_computation.15 | async-start | bytes 2621440 | tf_op jit(solution)/shard_map/all_gather | solution.py:109
  15.6 163.9 %all-gather.22.cloned.1.call-start = ((), (), s32[]{:S(2)}) async-start(), calls=%async_computation.18 | async-start | bytes 2621440 | tf_op jit(solution)/shard_map/all_gather | solution.py:174
  16.8 208.9 %all-gather.26.cloned.1.call-start = ((), (), s32[]{:S(2)}) async-start(), calls=%async_computation.22 | async-start | bytes 2621440 | tf_op jit(solution)/shard_map/all_gather | solution.py:174
  17.4 254.9 %all-gather.20.cloned.1.call-start = ((), (), s32[]{:S(2)}) async-start(), calls=%async_computation.16 | async-start | bytes 2621440 | tf_op jit(solution)/shard_map/all_gather | solution.py:110
  17.9 301.2 %all-gather.14.cloned.1.call-start = ((), (), s32[]{:S(2)}) async-start(), calls=%async_computation.12 | async-start | bytes 2621440 | tf_op jit(solution)/shard_map/all_gather | solution.py:110
  18.7 385.0 %all-gather.16.cloned.1.call-start = ((), (), s32[]{:S(2)}) async-start(), calls=%async_computation.13 | async-start | bytes 2359296 | tf_op jit(solution)/shard_map/all_gather | solution.py:116
  19.5 393.5 %all-gather.24.cloned.1.call-start = ((), (), s32[]{:S(2)}) async-start(), calls=%async_computation.20 | async-start | bytes 2359296 | tf_op jit(solution)/shard_map/all_gather | solution.py:178
  19.5 17.2 %collective-permute-start = (bf16[128,1024]{1,0:T(8,128)(2,1)S(1)}, bf16[128,1024]{1,0:T(8,128)(2,1)S(1)}, u32[]{:S(2)}, u32[]{:S(2)}) collective-permute-start(bf16[128,1024]{1,0:T(8,128)(2,1)S(1)} %copy-done.67), channel_id=1, source_target_pairs={{0,4},{4,0},{8,12},{12,8},{16,20},{20,16},{24,28},{28,24},{1,5},{5... | collective-permute-start | bytes 786440 | tf_op jit(solution)/shard_map/ppermute | solution.py:16
  20.2 463.0 %reduce-scatter.25.cloned.1.call-start = ((), (), s32[]{:S(2)}) async-start(), calls=%async_computation.26 | async-start | bytes 1179648 | tf_op jit(solution)/shard_map/reduce_scatter | solution.py:273
  35.6 210.0 %copy-start.23 = (bf16[1024,256]{1,0:T(8,128)(2,1)}, bf16[1024,256]{1,0:T(8,128)(2,1)S(1)}, u32[]{:S(2)}) copy-start(bf16[1024,256]{1,0:T(8,128)(2,1)S(1)} %all_gather.42) | copy-start | bytes 1572868
  36.9 14.2 %collective-permute-start.1 = (bf16[256,1024]{1,0:T(8,128)(2,1)S(1)}, bf16[256,1024]{1,0:T(8,128)(2,1)S(1)}, u32[]{:S(2)}, u32[]{:S(2)}) collective-permute-start(bf16[256,1024]{1,0:T(8,128)(2,1)S(1)} %maximum_select_fusion.2), channel_id=1, source_target_pairs={{0,8},{4,12},{8,0},{12,4},{16,24},{20,28},{24,16},{28,20},{1,9},{5... | collective-permute-start | bytes 1572872 | tf_op jit(solution)/shard_map/ppermute | solution.py:16
  39.6 197.1 %copy-start.12 = (pred[512,1024]{1,0:T(8,128)(4,1)}, pred[512,1024]{1,0:T(8,128)(4,1)S(1)}, u32[]{:S(2)}) copy-start(pred[512,1024]{1,0:T(8,128)(4,1)S(1)} %compare_and_fusion.1) | copy-start | bytes 1572868
  52.6 204.8 %collective-permute-start.2 = (bf16[512,1024]{1,0:T(8,128)(2,1)}, bf16[512,1024]{1,0:T(8,128)(2,1)}, u32[]{:S(2)}, u32[]{:S(2)}) collective-permute-start(bf16[512,1024]{1,0:T(8,128)(2,1)} %maximum_select_fusion.1), channel_id=1, source_target_pairs={{0,16},{4,20},{8,24},{12,28},{16,0},{20,4},{24,8},{28,12},{1,17},{... | collective-permute-start | bytes 3145736 | tf_op jit(solution)/shard_map/ppermute | solution.py:16
  245.5 239.3 %reduce-scatter.29.cloned.1.call-start = ((), (), s32[]{:S(2)}) async-start(), calls=%async_computation.28 | async-start | bytes 4718592 | tf_op jit(solution)/shard_map/reduce_scatter | solution.py:275
  356.2 194.2 %reduce-scatter.15.cloned.1.call-start = ((), (), s32[]{:S(2)}) async-start(), calls=%async_computation.19 | async-start | bytes 5242880 | tf_op jit(solution)/shard_map/reduce_scatter | solution.py:260
  387.3 242.7 %reduce-scatter.19.cloned.1.call-start = ((), (), s32[]{:S(2)}) async-start(), calls=%async_computation.23 | async-start | bytes 5242880 | tf_op jit(solution)/shard_map/reduce_scatter | solution.py:260
  403.6 305.9 %reduce-scatter.21.cloned.1.call-start = ((), (), s32[]{:S(2)}) async-start(), calls=%async_computation.24 | async-start | bytes 5242880 | tf_op jit(solution)/shard_map/reduce_scatter | solution.py:261
  419.6 369.4 %reduce-scatter.17.cloned.1.call-start = ((), (), s32[]{:S(2)}) async-start(), calls=%async_computation.21 | async-start | bytes 5242880 | tf_op jit(solution)/shard_map/reduce_scatter | solution.py:261
  433.8 435.8 %reduce-scatter.13.cloned.1.call-start = ((), (), s32[]{:S(2)}) async-start(), calls=%async_computation.17 | async-start | bytes 5242880 | tf_op jit(solution)/shard_map/reduce_scatter | solution.py:171
  442.2 506.8 %reduce-scatter.11.cloned.1.call-start = ((), (), s32[]{:S(2)}) async-start(), calls=%async_computation.14 | async-start | bytes 5242880 | tf_op jit(solution)/shard_map/reduce_scatter | solution.py:171
  449.2 550.7 %reduce-scatter.23.cloned.1.call-start = ((), (), s32[]{:S(2)}) async-start(), calls=%async_computation.25 | async-start | bytes 3538944 | tf_op jit(solution)/shard_map/reduce_scatter | solution.py:272
  457.9 597.3 %reduce-scatter.27.cloned.1.call-start = ((), (), s32[]{:S(2)}) async-start(), calls=%async_computation.27 | async-start | bytes 4718592 | tf_op jit(solution)/shard_map/reduce_scatter | solution.py:274
  467.3 162.7 %copy-start.84 = (f32[1024]{0:T(1024)S(1)}, f32[1024]{0:T(1024)}, u32[]{:S(2)}) copy-start(f32[1024]{0:T(1024)} %param.44) | copy-start | bytes 12292
  467.3 162.7 %copy-start.96 = (f32[256]{0:T(256)S(1)}, f32[256]{0:T(256)}, u32[]{:S(2)}) copy-start(f32[256]{0:T(256)} %copy-done.95) | copy-start | bytes 3076
  467.3 164.7 %copy-start.114 = (f32[256]{0:T(256)S(1)}, f32[256]{0:T(256)}, u32[]{:S(2)}) copy-start(f32[256]{0:T(256)} %copy-done.113) | copy-start | bytes 3076
  467.3 164.7 %copy-start.112 = (f32[256]{0:T(256)S(1)}, f32[256]{0:T(256)}, u32[]{:S(2)}) copy-start(f32[256]{0:T(256)} %copy-done.111) | copy-start | bytes 3076
  467.3 321.7 %copy-start.83 = (f32[1024]{0:T(1024)S(1)}, f32[1024]{0:T(1024)}, u32[]{:S(2)}) copy-start(f32[1024]{0:T(1024)} %param.46) | copy-start | bytes 12292
  467.3 321.6 %copy-start.107 = (f32[256]{0:T(256)S(1)}, f32[256]{0:T(256)}, u32[]{:S(2)}) copy-start(f32[256]{0:T(256)} %copy-done.106) | copy-start | bytes 3076
  467.4 321.6 %copy-start.109 = (f32[256]{0:T(256)S(1)}, f32[256]{0:T(256)}, u32[]{:S(2)}) copy-start(f32[256]{0:T(256)} %copy-done.108) | copy-start | bytes 3076
  839.1 216.1 %copy-start.117 = (f32[1024]{0:T(1024)}, f32[1024]{0:T(1024)S(1)}, u32[]{:S(2)}) copy-start(f32[1024]{0:T(1024)S(1)} %get-tuple-element.342) | copy-start | bytes 12292
  (134 other events, 2023.8 us)
Sparse Core Ops, SparseCore 0:
  9.9 29.0 all-gather.11
  41.2 45.9 all-gather.9
  88.7 44.6 all-gather.17
  134.8 44.6 all-gather.21
  180.9 44.6 all-gather.25
  227.6 44.6 all-gather.19
  274.5 44.6 all-gather.13
  321.0 26.6 all-gather.15
  349.6 27.8 all-gather.23
  380.5 36.0 reduce-scatter.24
  420.0 51.2 reduce-scatter.28
  473.6 76.7 reduce-scatter.14
  552.7 77.2 reduce-scatter.18
  632.2 77.2 reduce-scatter.20
  711.7 77.2 reduce-scatter.16
  791.2 78.3 reduce-scatter.12
  871.7 77.1 reduce-scatter.10
  953.1 46.7 reduce-scatter.22
  1003.8 51.3 reduce-scatter.26
